TPU v7x, 256 devices: a whole 4x4x8 slice. The times are simulated.
256 devices in a mesh: slab: 64 (over y, x, z_hi), pt: 4 (over z_lo, core).
Axes of the slice: x: 4, y: 4, z: 8 (z_hi: 4, z_lo: 2; z = z_hi * 2 + z_lo), core: 2. Of those that a mesh axis runs over, the one named last changes fastest.
Arguments:
- orbitals: bfloat16 [131072, 256], P('slab'), may hold values from -6 to 6
- potential: float32 [131072], P('slab'), may hold values from -1 to 1
- fit_matrix: bfloat16 [131072, 8192], P('slab', 'pt'), may hold values from -0.00390625 to 0.00390625
- owner_rows: int32 [4, 64, 64], P(None, 'slab'), may hold values from 0 to 2047, as said below
- owner_count: int32 [4, 64], replicated, may hold values from 0 to 64, as said below
Outputs:
- filtered: bfloat16 [131072, 256], P('slab')
Inputs may be any that keep to these rules, and one draw needn't show every extreme that they name: `owner_count`: for each block p the counts over slabs sum to 2048, and in every block some slab lists exactly 64 points. `owner_rows`: the listed entries (c < owner_count[p, s]) of slab s are distinct over all blocks p and slots c; the other entries are 0.
All inputs are finite; a program needn't handle non-finite values.
Results may differ from a plain program's by a relative error of at most 0.0054.
Values may be sent and summed in bfloat16 or wider, within the bound.
No kernel may reach another device: no remote copies, remote signals or barrier semaphores. Data moves between devices by JAX's collectives and lax.ppermute only.
A program may use at most 64 MiB of HBM per device.

v0:
```python
import jax
import jax.numpy as jnp
from jax import lax
from jax.sharding import PartitionSpec as P

DEG = 2
CZ = 8
NY = 8
NX = 32
stencil_coef = (-205.0 / 72.0, 8.0 / 5.0, -1.0 / 5.0, 8.0 / 315.0, -1.0 / 560.0)


def extended(cells, sides, width):
    for axis, dim in sides:
        count = lax.axis_size(axis)
        head = lax.slice_in_dim(cells, 0, width, axis=dim)
        tail = lax.slice_in_dim(cells, cells.shape[dim] - width, cells.shape[dim], axis=dim)
        cells = jnp.concatenate(
            [
                lax.ppermute(tail, axis, [(i, (i + 1) % count) for i in range(count)]),
                cells,
                lax.ppermute(head, axis, [((i + 1) % count, i) for i in range(count)]),
            ],
            axis=dim,
        )
    return cells


def plane_table():
    cell_ids = jnp.arange(NY * NX, dtype=jnp.int32)
    row_y = cell_ids // NX
    col_x = cell_ids % NX
    diff_y = (row_y[:, None] - row_y[None, :]) % NY
    diff_x = (col_x[:, None] - col_x[None, :]) % NX
    same_y = row_y[:, None] == row_y[None, :]
    same_x = col_x[:, None] == col_x[None, :]
    table = jnp.zeros((NY * NX, NY * NX), jnp.float32)
    for offset in range(1, 5):
        along_x = (same_y & (diff_x == offset % NX)).astype(jnp.float32) + (
            same_y & (diff_x == -offset % NX)
        ).astype(jnp.float32)
        along_y = (same_x & (diff_y == offset % NY)).astype(jnp.float32) + (
            same_x & (diff_y == -offset % NY)
        ).astype(jnp.float32)
        table = table + stencil_coef[offset] * (along_x + along_y)
    return table


def local_terms(vectors, potential):
    share_cols = vectors.shape[1]
    blocked = vectors.reshape(CZ, NY * NX, share_cols)
    padded = extended(blocked, (("slab", 0),), 4)
    center = blocked.astype(jnp.float32)
    in_plane = jnp.einsum(
        "pq,zqb->zpb",
        plane_table(),
        center,
        precision=lax.Precision.HIGHEST,
        preferred_element_type=jnp.float32,
    )
    summed = 3.0 * stencil_coef[0] * center + in_plane
    for offset in range(1, 5):
        upper = padded[4 + offset : 4 + offset + CZ].astype(jnp.float32)
        lower = padded[4 - offset : 4 - offset + CZ].astype(jnp.float32)
        summed = summed + stencil_coef[offset] * (upper + lower)
    kinetic = (-0.5 * summed).reshape(CZ * NY * NX, share_cols)
    return kinetic + potential[:, None] * center.reshape(CZ * NY * NX, share_cols)


def point_positions(count_row, capacity, point_total):
    inclusive = jnp.cumsum(count_row)
    point_ranks = jnp.arange(point_total, dtype=jnp.int32)
    before = (inclusive[None, :] <= point_ranks[:, None]).astype(jnp.int32)
    slab_of = jnp.sum(before, axis=1)
    base_count = jnp.sum(before * count_row[None, :], axis=1)
    return slab_of * capacity + point_ranks - base_count


def chebyshev(column_part, first_points, apply_op, next_points):
    previous = column_part
    current = column_part
    field_points = first_points
    for turn_number in range(DEG):
        applied = apply_op(current, field_points)
        scaled = applied - 3.5 * current.astype(jnp.float32)
        if turn_number == 0:
            upcoming = (scaled / 4.0).astype(jnp.bfloat16)
        else:
            upcoming = (0.5 * scaled - previous.astype(jnp.float32)).astype(jnp.bfloat16)
        previous, current = (current, upcoming)
        if turn_number + 1 < DEG:
            field_points = next_points(current)
    return current


def body(orbitals, potential, fit_matrix, owner_rows, owner_count):
    block_index = lax.axis_index("pt")
    capacity = owner_rows.shape[2]
    all_rows = owner_rows[:, 0, :]
    mine_rows = lax.dynamic_index_in_dim(all_rows, block_index, 0, keepdims=False)
    count_row = lax.dynamic_index_in_dim(owner_count, block_index, 0, keepdims=False)
    positions = point_positions(count_row, capacity, fit_matrix.shape[1])

    def gather_points(vectors):
        picked = jnp.take(vectors, mine_rows, axis=0)
        gathered = lax.all_gather(picked, "slab", axis=0, tiled=True)
        return jnp.take(gathered, positions, axis=0)

    psi_points = gather_points(orbitals)
    density = lax.dot_general(
        orbitals, psi_points, (((1,), (1,)), ((), ())), preferred_element_type=jnp.float32
    )
    kernel = (fit_matrix.astype(jnp.float32) * density).astype(jnp.bfloat16)

    def apply_whole(vectors, field_points):
        partial_value = jnp.dot(kernel, field_points, preferred_element_type=jnp.float32)
        exch_term = lax.psum(partial_value, "pt")
        return local_terms(vectors, potential) - exch_term

    return chebyshev(orbitals, psi_points, apply_whole, gather_points)


def solution(mesh):
    placed = (P("slab", None), P("slab"), P("slab", "pt"), P(None, "slab", None), P())
    return jax.shard_map(
        body, mesh=mesh, in_specs=placed, out_specs=P("slab", None), check_vma=False
    )
```

profile of v0, /device:TPU:1, one launch (start us, length us, event | category | flops | bytes accessed | tf_op | source)
XLA Modules:
  0.0 368.9 jit_solution(4444609752312211204)
XLA Ops:
  7.2 2.0 gather_fusion
  10.0 12.3 %copy.10 = bf16[2048,2048]{0,1:T(8,128)(2,1)} copy(bf16[2048,2048]{1,0:T(8,128)(2,1)} %param.11) | data formatting | bytes 16777216 | tf_op args[2]
  23.5 67.2 %all-gather.3.cloned.1.call-done = bf16[4096,256]{1,0:T(8,128)(2,1)} async-done(((bf16[64,256]{1,0:T(8,128)(2,1)}), bf16[4096,256]{1,0:T(8,128)(2,1)}) %all-gather.3.cloned.1.call-update) | async-done | bytes 2097168 | tf_op jit(solution)/shard_map/all_gather | solution.py:106
  90.7 8.5 %gather_fusion.1 = bf16[2048,256]{1,0:T(8,128)(2,1)S(1)} fusion(bf16[4096,256]{1,0:T(8,128)(2,1)} %all-gather.3.cloned.1.call-done, s32[2048]{0:T(1024)S(1)} %broadcast_clamp_fusion), kind=kCustom, calls=%fused_computation.1.clone | custom fusion | bytes 2105344 | tf_op jit(solution)/shard_map/jit(_take)/gather | solution.py:107
  99.3 4.8 %fusion = bf16[2048,2048]{0,1:T(8,128)(2,1)S(1)} fusion(bf16[2048,2048]{0,1:T(8,128)(2,1)} %copy.10, bf16[2048,256]{1,0:T(8,128)(2,1)S(1)} %copy-done.1, bf16[2048,256]{1,0:T(8,128)(2,1)S(1)} %gather_fusion.1, pred[2048]{0:T(1024)(128)(4,1)S(1)} %compare_and_fusion.15), kind=kOutput, calls=%fused_computation.5 | convolution fusion | flops 2160590848 | bytes 18876416 | tf_op jit(solution)/shard_map/dot_general | solution.py:110
  104.1 3.2 copy-done
  107.3 4.2 %fusion.37 = f32[2048,256]{1,0:T(8,128)} fusion(bf16[2048,2048]{0,1:T(8,128)(2,1)S(1)} %fusion, bf16[2048,256]{1,0:T(8,128)(2,1)S(1)} %gather_fusion.1, pred[2048]{0:T(1024)(128)(4,1)S(1)} %compare_and_fusion.15), kind=kOutput, calls=%fused_computation.102 | convolution fusion | flops 2148007936 | bytes 11536384 | tf_op jit(solution)/shard_map/dot_general | solution.py:116
  111.7 2.5 collective-permute-start.1
  114.3 5.3 %collective-permute-start = (bf16[4,256,256]{2,1,0:T(8,128)(2,1)S(1)}, bf16[4,256,256]{2,1,0:T(8,128)(2,1)S(1)}, u32[]{:S(2)}, u32[]{:S(2)}) collective-permute-start(bf16[4,256,256]{2,1,0:T(8,128)(2,1)S(1)} %bitcast.61), channel_id=1, source_target_pairs={{4,0},{8,4},{12,8},{16,12},{20,16},{24,20},{28,24},{32,28},{36,32}... | collective-permute-start | bytes 1572872 | tf_op jit(solution)/shard_map/ppermute | solution.py:22
  119.6 9.3 %collective-permute-done.1 = bf16[4,256,256]{2,1,0:T(8,128)(2,1)S(1)} collective-permute-done((bf16[4,256,256]{2,1,0:T(8,128)(2,1)S(1)}, bf16[4,256,256]{2,1,0:T(8,128)(2,1)S(1)}, u32[]{:S(2)}, u32[]{:S(2)}) %collective-permute-start.1) | collective-permute-done | bytes 524320 | tf_op jit(solution)/shard_map/ppermute | solution.py:20
  128.9 5.9 %collective-permute-done = bf16[4,256,256]{2,1,0:T(8,128)(2,1)S(1)} collective-permute-done((bf16[4,256,256]{2,1,0:T(8,128)(2,1)S(1)}, bf16[4,256,256]{2,1,0:T(8,128)(2,1)S(1)}, u32[]{:S(2)}, u32[]{:S(2)}) %collective-permute-start) | collective-permute-done | bytes 524320 | tf_op jit(solution)/shard_map/ppermute | solution.py:22
  134.8 5.7 %fusion.20 = f32[8,256,256]{2,1,0:T(8,128)} fusion(bf16[8,256,256]{2,1,0:T(8,128)(2,1)S(1)} %bitcast.59, bf16[4,256,256]{2,1,0:T(8,128)(2,1)S(1)} %collective-permute-done.1, bf16[4,256,256]{2,1,0:T(8,128)(2,1)S(1)} %collective-permute-done, s32[256]{0:T(256)S(1)} %get-tuple-element.17, s32[256]{0:T(256)S(1)} %get-tuple-element.18), kind=kOutput, calls=%fused_computation.44 | convolution fusion | flops 1633288192 | bytes 5246976 | tf_op jit(solution)/shard_map/pq,zqb->zpb/dot_general | solution.py:54
  140.5 46.3 %all-reduce.3.cloned.1.call-done = f32[2048,256]{1,0:T(8,128)} async-done(((f32[2048,256]{1,0:T(8,128)}), f32[2048,256]{1,0:T(8,128)}) %all-reduce.3.cloned.1.call-update) | async-done | bytes 2097168 | tf_op jit(solution)/shard_map/psum | solution.py:117
  186.8 2.8 fusion.9
  191.2 76.1 %all-gather.5.cloned.1.call-done = bf16[4096,256]{1,0:T(8,128)(2,1)} async-done(((bf16[64,256]{1,0:T(8,128)(2,1)}), bf16[4096,256]{1,0:T(8,128)(2,1)}) %all-gather.5.cloned.1.call-update) | async-done | bytes 2097168 | tf_op jit(solution)/shard_map/all_gather | solution.py:106
  267.3 8.5 %gather_fusion.3 = bf16[2048,256]{1,0:T(8,128)(2,1)S(1)} fusion(bf16[4096,256]{1,0:T(8,128)(2,1)} %all-gather.5.cloned.1.call-done, s32[2048]{0:T(1024)S(1)} %broadcast_clamp_fusion), kind=kCustom, calls=%fused_computation.3.clone | custom fusion | bytes 2105344 | tf_op jit(solution)/shard_map/jit(_take)/gather | solution.py:107
  275.8 7.5 %fusion.33 = f32[2048,256]{1,0:T(8,128)} fusion(bf16[2048,2048]{0,1:T(8,128)(2,1)} %copy-done, bf16[2048,256]{1,0:T(8,128)(2,1)S(1)} %gather_fusion.3, pred[2048]{0:T(1024)(128)(4,1)S(1)} %compare_and_fusion.15), kind=kOutput, calls=%fused_computation.73 | convolution fusion | flops 2148007936 | bytes 11536384 | tf_op jit(solution)/shard_map/dot_general | solution.py:116
  283.4 2.5 collective-permute-start.3
  285.9 5.3 %collective-permute-start.2 = (bf16[4,256,256]{2,1,0:T(8,128)(2,1)S(1)}, bf16[4,256,256]{2,1,0:T(8,128)(2,1)S(1)}, u32[]{:S(2)}, u32[]{:S(2)}) collective-permute-start(bf16[4,256,256]{2,1,0:T(8,128)(2,1)S(1)} %bitcast.63), channel_id=1, source_target_pairs={{4,0},{8,4},{12,8},{16,12},{20,16},{24,20},{28,24},{32,28},{36,32}... | collective-permute-start | bytes 1572872 | tf_op jit(solution)/shard_map/ppermute | solution.py:22
  291.3 9.3 %collective-permute-done.3 = bf16[4,256,256]{2,1,0:T(8,128)(2,1)S(1)} collective-permute-done((bf16[4,256,256]{2,1,0:T(8,128)(2,1)S(1)}, bf16[4,256,256]{2,1,0:T(8,128)(2,1)S(1)}, u32[]{:S(2)}, u32[]{:S(2)}) %collective-permute-start.3) | collective-permute-done | bytes 524320 | tf_op jit(solution)/shard_map/ppermute | solution.py:20
  300.6 6.0 %collective-permute-done.2 = bf16[4,256,256]{2,1,0:T(8,128)(2,1)S(1)} collective-permute-done((bf16[4,256,256]{2,1,0:T(8,128)(2,1)S(1)}, bf16[4,256,256]{2,1,0:T(8,128)(2,1)S(1)}, u32[]{:S(2)}, u32[]{:S(2)}) %collective-permute-start.2) | collective-permute-done | bytes 524320 | tf_op jit(solution)/shard_map/ppermute | solution.py:22
  306.5 4.7 %fusion.15 = f32[8,256,256]{2,1,0:T(8,128)} fusion(bf16[8,256,256]{2,1,0:T(8,128)(2,1)S(1)} %bitcast.60, bf16[4,256,256]{2,1,0:T(8,128)(2,1)S(1)} %collective-permute-done.3, bf16[4,256,256]{2,1,0:T(8,128)(2,1)S(1)} %collective-permute-done.2, s32[256]{0:T(256)S(1)} %get-tuple-element.17, s32[256]{0:T(256)S(1)} %get-tuple-element.18), kind=kOutput, calls=%fused_computation.38 | convolution fusion | flops 1633288192 | bytes 5246976 | tf_op jit(solution)/shard_map/pq,zqb->zpb/dot_general | solution.py:54
  311.2 47.2 %all-reduce.5.cloned.1.call-done = f32[2048,256]{1,0:T(8,128)} async-done(((f32[2048,256]{1,0:T(8,128)}), f32[2048,256]{1,0:T(8,128)}) %all-reduce.5.cloned.1.call-update) | async-done | bytes 2097168 | tf_op jit(solution)/shard_map/psum | solution.py:117
  358.4 3.9 %fusion.10 = bf16[2048,256]{1,0:T(8,128)(2,1)} fusion(bf16[2048,256]{1,0:T(8,128)(2,1)S(1)} %copy-done.1, f32[2048,256]{1,0:T(8,128)} %all-reduce.5.cloned.1.call-done, bf16[2048,256]{1,0:T(8,128)(2,1)S(1)} %fusion.9, f32[8,256,256]{2,1,0:T(8,128)} %fusion.15, f32[2048]{0:T(1024)S(1)} %copy-done.2), kind=kLoop, calls=%fused_computation.32 | loop fusion | flops 5242880 | bytes 7348224 | tf_op jit(solution)/shard_map/convert_element_type | solution.py:89
  (28 shorter events, 4.5 us)
Async XLA Ops:
  6.5 84.2 %all-gather.3.cloned.1.call-start = ((), (), s32[]{:S(2)}) async-start(), calls=%async_computation | async-start | bytes 2129920 | tf_op jit(solution)/shard_map/all_gather | solution.py:106
  9.9 176.8 %all-reduce.3.cloned.1.call-start = ((), (), s32[]{:S(2)}) async-start(), calls=%async_computation.1 | async-start | bytes 4194304 | tf_op jit(solution)/shard_map/psum | solution.py:117
  23.5 75.7 %copy-start.1 = (bf16[2048,256]{1,0:T(8,128)(2,1)S(1)}, bf16[2048,256]{1,0:T(8,128)(2,1)}, u32[]{:S(2)}) copy-start(bf16[2048,256]{1,0:T(8,128)(2,1)} %param.9) | copy-start | bytes 3145732
  104.1 3.2 copy-start
  111.6 155.7 %all-gather.5.cloned.1.call-start = ((), (), s32[]{:S(2)}) async-start(), calls=%async_computation.2 | async-start | bytes 2129920 | tf_op jit(solution)/shard_map/all_gather | solution.py:106
  111.7 17.2 %collective-permute-start.1 = (bf16[4,256,256]{2,1,0:T(8,128)(2,1)S(1)}, bf16[4,256,256]{2,1,0:T(8,128)(2,1)S(1)}, u32[]{:S(2)}, u32[]{:S(2)}) collective-permute-start(bf16[4,256,256]{2,1,0:T(8,128)(2,1)S(1)} %bitcast.62), channel_id=1, source_target_pairs={{0,4},{4,8},{8,12},{12,16},{16,20},{20,24},{24,28},{28,32},{32,36}... | collective-permute-start | bytes 1572872 | tf_op jit(solution)/shard_map/ppermute | solution.py:20
  114.3 20.5 %collective-permute-start = (bf16[4,256,256]{2,1,0:T(8,128)(2,1)S(1)}, bf16[4,256,256]{2,1,0:T(8,128)(2,1)S(1)}, u32[]{:S(2)}, u32[]{:S(2)}) collective-permute-start(bf16[4,256,256]{2,1,0:T(8,128)(2,1)S(1)} %bitcast.61), channel_id=1, source_target_pairs={{4,0},{8,4},{12,8},{16,12},{20,16},{24,20},{28,24},{32,28},{36,32}... | collective-permute-start | bytes 1572872 | tf_op jit(solution)/shard_map/ppermute | solution.py:22
  134.8 52.0 %copy-start.2 = (f32[2048]{0:T(1024)S(1)}, f32[2048]{0:T(1024)}, u32[]{:S(2)}) copy-start(f32[2048]{0:T(1024)} %param.10) | copy-start | bytes 24580
  191.0 167.4 %all-reduce.5.cloned.1.call-start = ((), (), s32[]{:S(2)}) async-start(), calls=%async_computation.3 | async-start | bytes 4194304 | tf_op jit(solution)/shard_map/psum | solution.py:117
  283.4 17.2 %collective-permute-start.3 = (bf16[4,256,256]{2,1,0:T(8,128)(2,1)S(1)}, bf16[4,256,256]{2,1,0:T(8,128)(2,1)S(1)}, u32[]{:S(2)}, u32[]{:S(2)}) collective-permute-start(bf16[4,256,256]{2,1,0:T(8,128)(2,1)S(1)} %bitcast.64), channel_id=1, source_target_pairs={{0,4},{4,8},{8,12},{12,16},{16,20},{20,24},{24,28},{28,32},{32,36}... | collective-permute-start | bytes 1572872 | tf_op jit(solution)/shard_map/ppermute | solution.py:20
  285.9 20.6 %collective-permute-start.2 = (bf16[4,256,256]{2,1,0:T(8,128)(2,1)S(1)}, bf16[4,256,256]{2,1,0:T(8,128)(2,1)S(1)}, u32[]{:S(2)}, u32[]{:S(2)}) collective-permute-start(bf16[4,256,256]{2,1,0:T(8,128)(2,1)S(1)} %bitcast.63), channel_id=1, source_target_pairs={{4,0},{8,4},{12,8},{16,12},{20,16},{24,20},{28,24},{32,28},{36,32}... | collective-permute-start | bytes 1572872 | tf_op jit(solution)/shard_map/ppermute | solution.py:22
Sparse Core Ops, SparseCore 0:
  10.6 80.0 all-gather.2
  111.7 74.9 all-reduce.2
  191.1 76.1 all-gather.4
  283.4 74.9 all-reduce.4
where the time goes:
time: 369 us
  waiting for transfers between devices  267 us (72%)
  local copies, waits for them, and re-layouts  36.2 us (10%)
  matrix products  27 us (7%)
  starting transfers between devices  16.1 us (4%)
  between operations  13.2 us (4%)
  other arithmetic  9.22 us (2%)
    all_gather x2, waiting for transfers between devices, gather_points(): gathered = lax.all_gather(picked, 'slab', axis=0, tiled=True)  143 us
    psum x2, waiting for transfers between devices, apply_whole(): exch_term = lax.psum(partial_value, 'pt')  93.5 us
    ppermute x2, waiting for transfers between devices, extended(): lax.ppermute(tail, axis, [(i, (i + 1) % count) for i in range(count)])  18.6 us
    gather x2, local copies, waits for them, and re-layouts, gather_points(): return jnp.take(gathered, positions, axis=0)  17 us
    unnamed x7, local copies, waits for them, and re-layouts  15.5 us
    ppermute x2, waiting for transfers between devices, extended(): lax.ppermute(head, axis, [((i + 1) % count, i) for i in range(count)])  11.9 us
    dot_general x2, matrix products, apply_whole(): jnp.dot(kernel, field_points, preferred_element_type=jnp.float32)  11.7 us
    ppermute x2, starting transfers between devices, extended(): lax.ppermute(head, axis, [((i + 1) % count, i) for i in range(count)])  10.7 us
  transfers between devices with their start and end apart: 8, of which 8 were waited for; matrix products, arithmetic and copies ran while one was open for 7% of the time, Pallas kernels for 0%

commit v1 on v0

--- a/solution.py
+++ b/solution.py
@@ -113,8 +113,12 @@
     kernel = (fit_matrix.astype(jnp.float32) * density).astype(jnp.bfloat16)
 
     def apply_whole(vectors, field_points):
+
+        def wrap_strips_all(original, chip_axis):
+            return lax.all_gather(original, axis_name=chip_axis).sum(axis=0)
+
         partial_value = jnp.dot(kernel, field_points, preferred_element_type=jnp.float32)
-        exch_term = lax.psum(partial_value, "pt")
+        exch_term = wrap_strips_all(partial_value, "pt")
         return local_terms(vectors, potential) - exch_term
 
     return chebyshev(orbitals, psi_points, apply_whole, gather_points)

time: 369 us -> 423 us (1.15)
  waiting for transfers between devices: 267 us -> 316 us
  other arithmetic: 9.22 us -> 20.3 us
  starting transfers between devices: 16.1 us -> 10.3 us
    all_gather x0 -> x2, waiting for transfers between devices: none -> 139 us  [wrap_strips_all(): return lax.all_gather(original, axis_name=chip_axis).sum(axis=0)]
    psum x2 -> x0, waiting for transfers between devices: 93.5 us -> none  [apply_whole(): exch_term = lax.psum(partial_value, 'pt')]
    ppermute x2, waiting for transfers between devices: 11.9 us -> 38.3 us  [extended(): lax.ppermute(head, axis, [((i + 1) % count, i) for i in range(count)])]
    ppermute x2, waiting for transfers between devices: 18.6 us -> 0.01 us  [extended(): lax.ppermute(tail, axis, [(i, (i + 1) % count) for i in range(count)])]
    reduce_sum x0 -> x2, other arithmetic: none -> 11.1 us  [wrap_strips_all(): return lax.all_gather(original, axis_name=chip_axis).sum(axis=0)]
    ppermute x2, starting transfers between devices: 5.08 us -> 0.01 us  [extended(): lax.ppermute(tail, axis, [(i, (i + 1) % count) for i in range(count)])]
    all_gather x2, waiting for transfers between devices: 143 us -> 139 us  [gather_points(): gathered = lax.all_gather(picked, 'slab', axis=0, tiled=True)]
  transfers between devices with their start and end apart: 8 -> 8, of which waited for: 8 -> 6; matrix products, arithmetic and copies ran while one was open for 7% -> 6% of each run, Pallas kernels for 0% -> 0%
where the time goes in v1:
time: 423 us
  waiting for transfers between devices  316 us (75%)
  local copies, waits for them, and re-layouts  36.2 us (9%)
  matrix products  26.9 us (6%)
  other arithmetic  20.3 us (5%)
  between operations  13.2 us (3%)
  starting transfers between devices  10.3 us (2%)
    all_gather x2, waiting for transfers between devices, gather_points(): gathered = lax.all_gather(picked, 'slab', axis=0, tiled=True)  139 us
    all_gather x2, waiting for transfers between devices, wrap_strips_all(): return lax.all_gather(original, axis_name=chip_axis).sum(axis=0)  139 us
    ppermute x2, waiting for transfers between devices, extended(): lax.ppermute(head, axis, [((i + 1) % count, i) for i in range(count)])  38.3 us
    gather x2, local copies, waits for them, and re-layouts, gather_points(): return jnp.take(gathered, positions, axis=0)  17 us
    unnamed x7, local copies, waits for them, and re-layouts  15.5 us
    dot_general x2, matrix products, apply_whole(): jnp.dot(kernel, field_points, preferred_element_type=jnp.float32)  11.7 us
    reduce_sum x2, other arithmetic, wrap_strips_all(): return lax.all_gather(original, axis_name=chip_axis).sum(axis=0)  11.1 us
    dot_general x2, matrix products, local_terms(): jnp.einsum('pq,zqb->zpb', plane_table(), center, precision=lax.Precision....  10.4 us
  transfers between devices with their start and end apart: 8, of which 6 were waited for; matrix products, arithmetic and copies ran while one was open for 6% of the time, Pallas kernels for 0%

profile of v1, /device:TPU:1, one launch (start us, length us, event | category | flops | bytes accessed | tf_op | source)
XLA Modules:
  0.0 422.8 jit_solution(12359619489950337764)
XLA Ops:
  7.2 2.0 gather_fusion
  9.2 0.7 broadcast_select_fusion.4
  11.0 12.3 %copy.10 = bf16[2048,2048]{0,1:T(8,128)(2,1)} copy(bf16[2048,2048]{1,0:T(8,128)(2,1)} %param.11) | data formatting | bytes 16777216 | tf_op args[2]
  23.5 67.2 %all-gather.7.cloned.1.call-done = bf16[4096,256]{1,0:T(8,128)(2,1)} async-done(((bf16[64,256]{1,0:T(8,128)(2,1)}), bf16[4096,256]{1,0:T(8,128)(2,1)}) %all-gather.7.cloned.1.call-update) | async-done | bytes 2097168 | tf_op jit(solution)/shard_map/all_gather | solution.py:106
  90.7 8.5 %gather_fusion.1 = bf16[2048,256]{1,0:T(8,128)(2,1)S(1)} fusion(bf16[4096,256]{1,0:T(8,128)(2,1)} %all-gather.7.cloned.1.call-done, s32[2048]{0:T(1024)S(1)} %broadcast_clamp_fusion), kind=kCustom, calls=%fused_computation.1.clone | custom fusion | bytes 2105344 | tf_op jit(solution)/shard_map/jit(_take)/gather | solution.py:107
  99.3 4.8 %fusion = bf16[2048,2048]{0,1:T(8,128)(2,1)S(1)} fusion(bf16[2048,2048]{0,1:T(8,128)(2,1)} %copy.10, bf16[2048,256]{1,0:T(8,128)(2,1)S(1)} %copy-done.1, bf16[2048,256]{1,0:T(8,128)(2,1)S(1)} %gather_fusion.1, pred[2048]{0:T(1024)(128)(4,1)S(1)} %compare_and_fusion.15), kind=kOutput, calls=%fused_computation.5 | convolution fusion | flops 2160590848 | bytes 18876416 | tf_op jit(solution)/shard_map/dot_general | solution.py:110
  104.1 3.2 copy-done
  107.3 4.2 fusion.37
  111.7 5.0 %collective-permute-start = (bf16[4,256,256]{2,1,0:T(8,128)(2,1)S(1)}, bf16[4,256,256]{2,1,0:T(8,128)(2,1)S(1)}, u32[]{:S(2)}, u32[]{:S(2)}) collective-permute-start(bf16[4,256,256]{2,1,0:T(8,128)(2,1)S(1)} %bitcast.66), channel_id=1, source_target_pairs={{4,0},{8,4},{12,8},{16,12},{20,16},{24,20},{28,24},{32,28},{36,32}... | collective-permute-start | bytes 1572872 | tf_op jit(solution)/shard_map/ppermute | solution.py:22
  116.7 19.1 %collective-permute-done = bf16[4,256,256]{2,1,0:T(8,128)(2,1)S(1)} collective-permute-done((bf16[4,256,256]{2,1,0:T(8,128)(2,1)S(1)}, bf16[4,256,256]{2,1,0:T(8,128)(2,1)S(1)}, u32[]{:S(2)}, u32[]{:S(2)}) %collective-permute-start) | collective-permute-done | bytes 524320 | tf_op jit(solution)/shard_map/ppermute | solution.py:22
  135.8 5.7 %fusion.20 = f32[8,256,256]{2,1,0:T(8,128)} fusion(bf16[8,256,256]{2,1,0:T(8,128)(2,1)S(1)} %bitcast.61, bf16[4,256,256]{2,1,0:T(8,128)(2,1)S(1)} %collective-permute-done.1, bf16[4,256,256]{2,1,0:T(8,128)(2,1)S(1)} %collective-permute-done, s32[256]{0:T(256)S(1)} %get-tuple-element.17, s32[256]{0:T(256)S(1)} %get-tuple-element.18), kind=kOutput, calls=%fused_computation.44 | convolution fusion | flops 1633288192 | bytes 5246976 | tf_op jit(solution)/shard_map/pq,zqb->zpb/dot_general | solution.py:54
  141.5 68.9 %all-gather.11.cloned.1.call-done = f32[8192,256]{1,0:T(8,128)} async-done(((f32[2048,256]{1,0:T(8,128)}), f32[8192,256]{1,0:T(8,128)}) %all-gather.11.cloned.1.call-update) | async-done | bytes 8388624 | tf_op jit(solution)/shard_map/all_gather | solution.py:118
  210.3 5.5 %reduce_sum.38 = f32[2048,256]{1,0:T(8,128)} reduce(f32[4,2048,256]{2,1,0:T(8,128)} %bitcast.63, f32[]{:T(128)} %constant.143.clone.1), dimensions={0}, to_apply=%region_3.6 | reduce | flops 1572864 | bytes 10485764 | tf_op jit(solution)/shard_map/reduce_sum | solution.py:118
  215.9 2.8 fusion.9
  218.7 0.7 gather_fusion.2
  220.3 71.7 %all-gather.9.cloned.1.call-done = bf16[4096,256]{1,0:T(8,128)(2,1)} async-done(((bf16[64,256]{1,0:T(8,128)(2,1)}), bf16[4096,256]{1,0:T(8,128)(2,1)}) %all-gather.9.cloned.1.call-update) | async-done | bytes 2097168 | tf_op jit(solution)/shard_map/all_gather | solution.py:106
  292.0 8.5 %gather_fusion.3 = bf16[2048,256]{1,0:T(8,128)(2,1)S(1)} fusion(bf16[4096,256]{1,0:T(8,128)(2,1)} %all-gather.9.cloned.1.call-done, s32[2048]{0:T(1024)S(1)} %broadcast_clamp_fusion), kind=kCustom, calls=%fused_computation.3.clone | custom fusion | bytes 2105344 | tf_op jit(solution)/shard_map/jit(_take)/gather | solution.py:107
  300.5 7.5 %fusion.33 = f32[2048,256]{1,0:T(8,128)} fusion(bf16[2048,2048]{0,1:T(8,128)(2,1)} %copy-done, bf16[2048,256]{1,0:T(8,128)(2,1)S(1)} %gather_fusion.3, pred[2048]{0:T(1024)(128)(4,1)S(1)} %compare_and_fusion.15), kind=kOutput, calls=%fused_computation.73 | convolution fusion | flops 2148007936 | bytes 11536384 | tf_op jit(solution)/shard_map/dot_general | solution.py:120
  308.1 5.0 %collective-permute-start.2 = (bf16[4,256,256]{2,1,0:T(8,128)(2,1)S(1)}, bf16[4,256,256]{2,1,0:T(8,128)(2,1)S(1)}, u32[]{:S(2)}, u32[]{:S(2)}) collective-permute-start(bf16[4,256,256]{2,1,0:T(8,128)(2,1)S(1)} %bitcast.68), channel_id=1, source_target_pairs={{4,0},{8,4},{12,8},{16,12},{20,16},{24,20},{28,24},{32,28},{36,32}... | collective-permute-start | bytes 1572872 | tf_op jit(solution)/shard_map/ppermute | solution.py:22
  313.1 19.1 %collective-permute-done.2 = bf16[4,256,256]{2,1,0:T(8,128)(2,1)S(1)} collective-permute-done((bf16[4,256,256]{2,1,0:T(8,128)(2,1)S(1)}, bf16[4,256,256]{2,1,0:T(8,128)(2,1)S(1)}, u32[]{:S(2)}, u32[]{:S(2)}) %collective-permute-start.2) | collective-permute-done | bytes 524320 | tf_op jit(solution)/shard_map/ppermute | solution.py:22
  332.2 4.7 %fusion.15 = f32[8,256,256]{2,1,0:T(8,128)} fusion(bf16[8,256,256]{2,1,0:T(8,128)(2,1)S(1)} %bitcast.62, bf16[4,256,256]{2,1,0:T(8,128)(2,1)S(1)} %collective-permute-done.3, bf16[4,256,256]{2,1,0:T(8,128)(2,1)S(1)} %collective-permute-done.2, s32[256]{0:T(256)S(1)} %get-tuple-element.17, s32[256]{0:T(256)S(1)} %get-tuple-element.18), kind=kOutput, calls=%fused_computation.38 | convolution fusion | flops 1633288192 | bytes 5246976 | tf_op jit(solution)/shard_map/pq,zqb->zpb/dot_general | solution.py:54
  337.0 69.8 %all-gather.13.cloned.1.call-done = f32[8192,256]{1,0:T(8,128)} async-done(((f32[2048,256]{1,0:T(8,128)}), f32[8192,256]{1,0:T(8,128)}) %all-gather.13.cloned.1.call-update) | async-done | bytes 8388624 | tf_op jit(solution)/shard_map/all_gather | solution.py:118
  406.7 5.6 %reduce_sum.39 = f32[2048,256]{1,0:T(8,128)} reduce(f32[4,2048,256]{2,1,0:T(8,128)} %bitcast.64, f32[]{:T(128)} %constant.143.clone.1), dimensions={0}, to_apply=%region_4.7 | reduce | flops 1572864 | bytes 10485764 | tf_op jit(solution)/shard_map/reduce_sum | solution.py:118
  412.3 3.9 fusion.10
  (30 shorter events, 3.1 us)
Async XLA Ops:
  6.5 84.2 %all-gather.7.cloned.1.call-start = ((), (), s32[]{:S(2)}) async-start(), calls=%async_computation | async-start | bytes 2129920 | tf_op jit(solution)/shard_map/all_gather | solution.py:106
  9.9 200.4 %all-gather.11.cloned.1.call-start = ((), (), s32[]{:S(2)}) async-start(), calls=%async_computation.2 | async-start | bytes 10485760 | tf_op jit(solution)/shard_map/all_gather | solution.py:118
  23.5 75.7 %copy-start.1 = (bf16[2048,256]{1,0:T(8,128)(2,1)S(1)}, bf16[2048,256]{1,0:T(8,128)(2,1)}, u32[]{:S(2)}) copy-start(bf16[2048,256]{1,0:T(8,128)(2,1)} %param.9) | copy-start | bytes 3145732
  104.1 3.2 copy-start
  111.6 180.4 %all-gather.9.cloned.1.call-start = ((), (), s32[]{:S(2)}) async-start(), calls=%async_computation.1 | async-start | bytes 2129920 | tf_op jit(solution)/shard_map/all_gather | solution.py:106
  111.7 24.1 %collective-permute-start = (bf16[4,256,256]{2,1,0:T(8,128)(2,1)S(1)}, bf16[4,256,256]{2,1,0:T(8,128)(2,1)S(1)}, u32[]{:S(2)}, u32[]{:S(2)}) collective-permute-start(bf16[4,256,256]{2,1,0:T(8,128)(2,1)S(1)} %bitcast.66), channel_id=1, source_target_pairs={{4,0},{8,4},{12,8},{16,12},{20,16},{24,20},{28,24},{32,28},{36,32}... | collective-permute-start | bytes 1572872 | tf_op jit(solution)/shard_map/ppermute | solution.py:22
  116.7 19.1 %collective-permute-start.1 = (bf16[4,256,256]{2,1,0:T(8,128)(2,1)S(1)}, bf16[4,256,256]{2,1,0:T(8,128)(2,1)S(1)}, u32[]{:S(2)}, u32[]{:S(2)}) collective-permute-start(bf16[4,256,256]{2,1,0:T(8,128)(2,1)S(1)} %bitcast.65), channel_id=1, source_target_pairs={{0,4},{4,8},{8,12},{12,16},{16,20},{20,24},{24,28},{28,32},{32,36}... | collective-permute-start | bytes 1572872 | tf_op jit(solution)/shard_map/ppermute | solution.py:20
  210.3 5.5 %copy-start.2 = (f32[2048]{0:T(1024)S(1)}, f32[2048]{0:T(1024)}, u32[]{:S(2)}) copy-start(f32[2048]{0:T(1024)} %param.10) | copy-start | bytes 24580
  220.1 186.6 %all-gather.13.cloned.1.call-start = ((), (), s32[]{:S(2)}) async-start(), calls=%async_computation.3 | async-start | bytes 10485760 | tf_op jit(solution)/shard_map/all_gather | solution.py:118
  308.1 24.1 %collective-permute-start.2 = (bf16[4,256,256]{2,1,0:T(8,128)(2,1)S(1)}, bf16[4,256,256]{2,1,0:T(8,128)(2,1)S(1)}, u32[]{:S(2)}, u32[]{:S(2)}) collective-permute-start(bf16[4,256,256]{2,1,0:T(8,128)(2,1)S(1)} %bitcast.68), channel_id=1, source_target_pairs={{4,0},{8,4},{12,8},{16,12},{20,16},{24,20},{28,24},{32,28},{36,32}... | collective-permute-start | bytes 1572872 | tf_op jit(solution)/shard_map/ppermute | solution.py:22
  313.1 19.1 %collective-permute-start.3 = (bf16[4,256,256]{2,1,0:T(8,128)(2,1)S(1)}, bf16[4,256,256]{2,1,0:T(8,128)(2,1)S(1)}, u32[]{:S(2)}, u32[]{:S(2)}) collective-permute-start(bf16[4,256,256]{2,1,0:T(8,128)(2,1)S(1)} %bitcast.67), channel_id=1, source_target_pairs={{0,4},{4,8},{8,12},{12,16},{16,20},{20,24},{24,28},{28,32},{32,36}... | collective-permute-start | bytes 1572872 | tf_op jit(solution)/shard_map/ppermute | solution.py:20
Sparse Core Ops, SparseCore 0:
  10.6 80.0 all-gather.6
  111.7 98.6 all-gather.10
  220.2 71.7 all-gather.8
  308.1 98.5 all-gather.12
